TPU v7x, 32 devices: a whole 2x2x4 slice. The times are simulated.
32 devices in a mesh: parts: 2 (over y), dp: 4 (over z), tensor: 4 (over x, core).
Axes of the slice: x: 2, y: 2, z: 4, core: 2. Of those that a mesh axis runs over, the one named last changes fastest.
Arguments:
- prompt_kv: bfloat16 [2, 14336, 8, 128], P(None, ('parts', 'dp'), 'tensor'), parts along dimension 1, may hold values from -12 to 12
- gen_kv: bfloat16 [64, 2, 128, 8, 128], P(('parts', 'dp'), None, None, 'tensor'), parts along dimension 0, may hold values from -17 to 17
- queries: bfloat16 [2, 64, 64, 128], P(None, ('parts', 'dp'), 'tensor'), parts along dimension 1, may hold values from -24 to 24
- new_kv: bfloat16 [2, 2, 64, 8, 128], P(None, None, ('parts', 'dp'), 'tensor'), parts along dimension 2, may hold values from -48 to 48
- ancestors: int32 [64], P(('parts', 'dp')), parts along dimension 0, may hold values from 0 to 31, as said below
- prior_twist: float32 [64], P(('parts', 'dp')), parts along dimension 0, may hold values from -290 to 6
- twist_vec: float32 [64, 128], P('tensor'), may hold values from -1 to 1
Outputs:
- attended: bfloat16 [2, 64, 64, 128], P(None, ('parts', 'dp'), 'tensor'), parts along dimension 1
- log_weights: float32 [64], P(('parts', 'dp')), parts along dimension 0
There are 2 independent parts, one for each index of `parts`. A program takes and returns all parts, laid end to end along the dimension named above; an argument that names none is the same for every part. Nothing has to cross between parts.
Inputs may be any that keep to these rules, and one draw needn't show every extreme that they name: Duplicates are allowed. Among the 8 particles of one device (equal p // 8) at most 4 have ancestors held by one same device (equal ancestors // 8), and every device has exactly 4 from some device.
All inputs are finite; a program needn't handle non-finite values.
Results may differ from a plain program's by a relative error of at most 0.0017.
Values may be sent and summed in bfloat16 or wider, within the bound.
A program may use at most 128 MiB of HBM per device.

v0:
```python
import math
import jax
import jax.numpy as jnp
from jax import lax
from jax.sharding import PartitionSpec as P


def join_states(left_state, right_state):
    largest = jnp.maximum(left_state[0], right_state[0])
    left_scale = jnp.exp(left_state[0] - largest)
    right_scale = jnp.exp(right_state[0] - largest)
    return (
        largest,
        left_state[1] * left_scale + right_state[1] * right_scale,
        left_state[2] * left_scale[..., None] + right_state[2] * right_scale[..., None],
    )


def fold_blocks(moments, totals, weighted, along):
    largest = jnp.max(moments, axis=along)
    scale_each = jnp.exp(moments - jnp.expand_dims(largest, along))
    return (
        largest,
        jnp.sum(totals * scale_each, axis=along),
        jnp.sum(weighted * scale_each[..., None], axis=along),
    )


def block_state(scores, values, pattern):
    largest = jnp.max(scores, axis=-1)
    exponent = jnp.exp(scores - largest[..., None])
    weighted = jnp.einsum(
        pattern, exponent.astype(jnp.bfloat16), values, preferred_element_type=jnp.float32
    )
    return (largest, jnp.sum(exponent, axis=-1), weighted)


def prompt_states(query_rows, prompt_kv, kv_count, scaling):
    row_count, head_count, head_size = query_rows.shape
    group_size = head_count // kv_count
    per_block = math.gcd(row_count, 256)
    blocked = query_rows.reshape(row_count // per_block, per_block, kv_count, group_size, head_size)
    key_rows = prompt_kv[0]
    values = prompt_kv[1]

    def attend_block(query_block):
        scores = (
            jnp.einsum("pcgd,kcd->pcgk", query_block, key_rows, preferred_element_type=jnp.float32)
            * scaling
        )
        return block_state(scores, values, "pcgk,kcd->pcgd")

    largest, totals, weighted = lax.map(attend_block, blocked)
    return (
        largest.reshape(row_count, head_count),
        totals.reshape(row_count, head_count),
        weighted.reshape(row_count, head_count, head_size),
    )


def per_device(prompt_kv, gen_kv, queries, new_kv, ancestors, prior_twist, twist_vec):
    step_count, local_count, head_count, head_size = queries.shape
    kv_count = prompt_kv.shape[2]
    group_size = head_count // kv_count
    scaling = 1.0 / math.sqrt(head_size)
    devices = lax.axis_size("dp")
    capacity = max(2, (2 * local_count + devices - 1) // devices)
    slot_total = devices * capacity
    source = ancestors // local_count
    offset = ancestors % local_count
    places = jnp.arange(local_count)
    earlier = (source[:, None] == source[None, :]) & (places[None, :] < places[:, None])
    arrival_rank = jnp.sum(earlier.astype(jnp.int32), axis=1)
    slot_index = source * capacity + arrival_rank
    slot_match = jnp.arange(slot_total)[:, None] == slot_index[None, :]
    wanted = jnp.sum(jnp.where(slot_match, offset[None, :] + 1, 0), axis=1) - 1
    requests_in = lax.all_to_all(
        wanted.reshape(devices, capacity), "dp", split_axis=0, concat_axis=0, tiled=True
    )
    picked = jnp.clip(requests_in, 0, local_count - 1).reshape(-1)
    every_prior = lax.all_gather(prior_twist, "dp", axis=0, tiled=True)
    twist_before = jnp.take(every_prior, ancestors, axis=0)
    split_query = queries.reshape(step_count, local_count, kv_count, group_size, head_size)
    sent_rows = jnp.take(gen_kv, picked, axis=0).reshape((devices, capacity) + gen_kv.shape[1:])
    arrived = lax.all_to_all(sent_rows, "dp", split_axis=0, concat_axis=0, tiled=True)
    resampled = jnp.take(arrived.reshape((slot_total,) + gen_kv.shape[1:]), slot_index, axis=0)
    cache_scores = (
        jnp.einsum(
            "spcgd,pkcd->spcgk", split_query, resampled[:, 0], preferred_element_type=jnp.float32
        )
        * scaling
    )
    largest, totals, weighted = block_state(cache_scores, resampled[:, 1], "spcgk,pkcd->spcgd")
    cached = (
        largest.reshape(step_count, local_count, head_count),
        totals.reshape(step_count, local_count, head_count),
        weighted.reshape(step_count, local_count, head_count, head_size),
    )
    new_scores = (
        jnp.einsum(
            "spcgd,tpcd->spcgt", split_query, new_kv[:, 0], preferred_element_type=jnp.float32
        )
        * scaling
    )
    positions = jnp.arange(step_count)
    allowed = positions[None, :] <= positions[:, None]
    new_scores = jnp.where(allowed[:, None, None, None, :], new_scores, -jnp.inf)
    largest, totals, weighted = block_state(new_scores, new_kv[:, 1], "spcgt,tpcd->spcgd")
    fresh_state = (
        largest.reshape(step_count, local_count, head_count),
        totals.reshape(step_count, local_count, head_count),
        weighted.reshape(step_count, local_count, head_count, head_size),
    )
    everyone = lax.all_gather(queries, "dp", axis=1, tiled=True)
    largest, totals, weighted = prompt_states(
        everyone.reshape(step_count * devices * local_count, head_count, head_size),
        prompt_kv,
        kv_count,
        scaling,
    )
    arrived_states = (
        lax.all_to_all(
            largest.reshape(step_count, devices, local_count, head_count),
            "dp",
            split_axis=1,
            concat_axis=1,
            tiled=True,
        ),
        lax.all_to_all(
            totals.reshape(step_count, devices, local_count, head_count),
            "dp",
            split_axis=1,
            concat_axis=1,
            tiled=True,
        ),
        lax.all_to_all(
            weighted.reshape(step_count, devices, local_count, head_count, head_size),
            "dp",
            split_axis=1,
            concat_axis=1,
            tiled=True,
        ),
    )
    prompt_state = fold_blocks(arrived_states[0], arrived_states[1], arrived_states[2], 1)
    joined = join_states(join_states(prompt_state, cached), fresh_state)
    attended = (joined[2] / joined[1][..., None]).astype(jnp.bfloat16)
    last_step = lax.optimization_barrier(attended[-1]).astype(jnp.float32)
    local_twist = jnp.sum(last_step * twist_vec, axis=(1, 2))
    twist_value = lax.psum(local_twist, "tensor")
    raw_weight = twist_value - twist_before
    largest_weight = lax.pmax(jnp.max(raw_weight), "dp")
    weight_mass = lax.psum(jnp.sum(jnp.exp(raw_weight - largest_weight)), "dp")
    normalizer = largest_weight + jnp.log(weight_mass)
    return (attended, raw_weight - normalizer)


def solution(mesh):
    placed = (
        P(None, ("parts", "dp"), "tensor", None),
        P(("parts", "dp"), None, None, "tensor", None),
        P(None, ("parts", "dp"), "tensor", None),
        P(None, None, ("parts", "dp"), "tensor", None),
        P(("parts", "dp")),
        P(("parts", "dp")),
        P("tensor", None),
    )
    return jax.shard_map(
        per_device,
        mesh=mesh,
        in_specs=placed,
        out_specs=(P(None, ("parts", "dp"), "tensor", None), P(("parts", "dp"))),
        check_vma=False,
    )
```

profile of v0, /device:TPU:0, one launch (start us, length us, event | category | flops | bytes accessed | tf_op | source)
XLA Modules:
  0.0 157.3 jit_solution(7130623179860953342)
XLA Ops:
  0.6 0.8 compare_select_fusion.3
  1.4 0.2 convert_reduce_fusion
  1.7 0.7 sub.106
  2.4 6.3 %all-to-all-start.2 = ((s32[4,1,4]{2,1,0:T(1,128)}), s32[4,1,4]{2,1,0:T(1,128)S(1)}, u32[]{:S(2)}, u32[]{:S(2)}) async-start(s32[4,1,4]{2,1,0:T(1,128)} %bitcast.10), calls=%async_computation.2 | async-start | bytes 4096 | tf_op jit(solution)/shard_map/all_to_all | solution.py:77
  8.7 14.6 %all_gather.6 = bf16[2,32,16,128]{3,2,1,0:T(8,128)(2,1)S(1)} all-gather(bf16[2,8,16,128]{3,2,1,0:T(8,128)(2,1)} %param.9), channel_id=1, replica_groups=mesh['parts'=2,'dp'=4,'tensor'=4] {'dp'}, dimensions={1}, use_global_device_ids=true | all-gather | bytes 327680 | tf_op jit(solution)/shard_map/all_gather | solution.py:114
  23.4 2.5 %fusion.38 = (bf16[1,1792,2,128]{3,2,1,0:T(2,128)(2,1)S(1)}, bf16[1,1792,2,128]{3,2,1,0:T(2,128)(2,1)S(1)}) fusion(bf16[2,1792,2,128]{3,2,1,0:T(2,128)(2,1)} %param.7), kind=kLoop, calls=%fused_computation.88 | loop fusion | bytes 3670016 | tf_op jit(solution)/shard_map/slice | solution.py:44
  25.9 4.1 %bitcast_reduce_fusion = (f32[64,2,8]{0,2,1:T(8,128)S(1)}, f32[2,1792,64,8]{1,2,3,0:T(8,128)}) fusion(bf16[64,2,8,128]{3,0,2,1:T(8,128)(2,1)S(1)} %bitcast.113, bf16[1,1792,2,128]{3,2,1,0:T(2,128)(2,1)S(1)} %get-tuple-element.35), kind=kOutput, calls=%fused_computation.4 | convolution fusion | flops 473431040 | bytes 8523776 | tf_op jit(solution)/shard_map/while/body/eval_jaxpr/pcgd,kcd->pcgk/dot_general | solution.py:48
  30.0 0.1 reshape_reshape.11
  30.1 0.1 copy.105
  30.2 4.4 %fusion.3 = f32[2,64,8,128]{3,1,2,0:T(8,128)S(1)} fusion(f32[2,1792,64,8]{1,2,3,0:T(8,128)} %get-tuple-element.48, f32[64,2,8]{0,2,1:T(8,128)S(1)} %get-tuple-element.47, bf16[1,1792,2,128]{3,2,1,0:T(2,128)(2,1)S(1)} %get-tuple-element.34), kind=kOutput, calls=%fused_computation.8 | convolution fusion | flops 475267072 | bytes 8785920 | tf_op jit(solution)/shard_map/while/body/eval_jaxpr/pcgk,kcd->pcgd/dot_general | solution.py:32
  34.6 0.7 reshape.241
  35.3 4.9 %all-to-all-start.1 = ((f32[4,1,256]{2,1,0:T(1,128)}), f32[4,1,256]{2,1,0:T(1,128)S(1)}, u32[]{:S(2)}, u32[]{:S(2)}) async-start(f32[4,1,256]{2,1,0:T(1,128)} %reshape.241), calls=%async_computation.1 | async-start | bytes 8192 | tf_op jit(solution)/shard_map/all_to_all | solution.py:122
  40.2 4.4 %fusion.1 = f32[64,2,8]{0,2,1:T(8,128)S(1)} fusion(f32[2,1792,64,8]{1,2,3,0:T(8,128)} %get-tuple-element.48, f32[64,2,8]{0,2,1:T(8,128)S(1)} %get-tuple-element.47), kind=kLoop, calls=%fused_computation.6 | loop fusion | flops 5504000 | bytes 7348224 | tf_op jit(solution)/shard_map/while/body/eval_jaxpr/reduce_sum | solution.py:35
  44.6 1.1 copy.104
  45.7 0.1 reshape_reshape.12
  45.8 0.1 copy.121
  45.9 0.7 reshape.243
  46.6 5.1 %all-to-all-start.4 = ((f32[4,1,256]{2,1,0:T(1,128)}), f32[4,1,256]{2,1,0:T(1,128)S(1)}, u32[]{:S(2)}, u32[]{:S(2)}) async-start(f32[4,1,256]{2,1,0:T(1,128)} %reshape.243), calls=%async_computation.4 | async-start | bytes 8192 | tf_op jit(solution)/shard_map/all_to_all | solution.py:129
  51.8 5.5 %all-to-all-done.4 = f32[4,1,256]{2,1,0:T(1,128)S(1)} async-done(((f32[4,1,256]{2,1,0:T(1,128)}), f32[4,1,256]{2,1,0:T(1,128)S(1)}, u32[]{:S(2)}, u32[]{:S(2)}) %all-to-all-start.4) | async-done | bytes 4128 | tf_op jit(solution)/shard_map/all_to_all | solution.py:129
  57.3 4.1 %all-to-all-start = ((f32[2,4,8,16,128]{4,3,2,0,1:T(8,128)}), f32[2,4,8,16,128]{4,3,2,0,1:T(8,128)}, u32[]{:S(2)}, u32[]{:S(2)}) async-start(f32[2,4,8,16,128]{4,3,2,0,1:T(8,128)} %copy.104), calls=%async_computation | async-start | bytes 1048576 | tf_op jit(solution)/shard_map/all_to_all | solution.py:136
  61.4 5.1 %gather_fusion = bf16[16,2,128,2,128]{4,3,2,1,0:T(2,128)(2,1)S(1)} fusion(bf16[8,2,128,2,128]{4,3,2,1,0:T(2,128)(2,1)S(1)} %copy-done, s32[1024]{0:T(1024)S(1)} %pad_clamp_fusion.2), kind=kCustom, calls=%fused_computation | custom fusion | bytes 4194368 | tf_op jit(solution)/shard_map/jit(_take)/gather | solution.py:84
  66.5 1.7 %copy_select_fusion = bf16[4,4,2,128,2,128]{5,3,4,2,1,0:T(8,128)(2,1)} fusion(bf16[4,4,2,128,2,128]{5,4,3,2,1,0:T(2,128)(2,1)S(1)} %bitcast.110, pred[4,4]{1,0:T(4,128)(4,1)S(1)} %compare_and_fusion), kind=kLoop, calls=%fused_computation.11 | loop fusion | flops 1048576 | bytes 4194320 | tf_op jit(solution)/shard_map/jit(_take)/select_n | solution.py:84
  68.2 3.6 %all-to-all-done = f32[2,4,8,16,128]{4,3,2,0,1:T(8,128)} async-done(((f32[2,4,8,16,128]{4,3,2,0,1:T(8,128)}), f32[2,4,8,16,128]{4,3,2,0,1:T(8,128)}, u32[]{:S(2)}, u32[]{:S(2)}) %all-to-all-start) | async-done | bytes 524320 | tf_op jit(solution)/shard_map/all_to_all | solution.py:136
  71.9 3.6 %all-to-all-start.3 = ((bf16[4,4,2,128,2,128]{5,3,4,2,1,0:T(8,128)(2,1)}), bf16[4,4,2,128,2,128]{5,3,4,2,1,0:T(8,128)(2,1)S(1)}, u32[]{:S(2)}, u32[]{:S(2)}) async-start(bf16[4,4,2,128,2,128]{5,3,4,2,1,0:T(8,128)(2,1)} %copy_select_fusion), calls=%async_computation.3 | async-start | bytes 4194304 | tf_op jit(solution)/shard_map/all_to_all | solution.py:85
  75.5 0.4 fusion.40
  76.2 0.6 dynamic-slice
  77.5 0.2 dynamic-update-slice
  77.7 31.2 %all-reduce = f32[32]{0:T(128)S(1)} all-reduce(f32[32]{0:T(128)S(1)} %dynamic-update-slice), channel_id=1, replica_groups=mesh['parts'=2,'dp'=4,'tensor'=4] {'dp'}, use_global_device_ids=true, to_apply=%add | all-reduce | flops 32 | bytes 256
  109.0 0.2 convolution_bitcast_fusion.1
  109.2 0.5 broadcast.204
  109.7 0.7 reduce.4
  110.4 0.7 reduce.5
  111.2 1.3 multiply_reduce_fusion
  112.5 4.7 %all-to-all-done.3 = bf16[4,4,2,128,2,128]{5,3,4,2,1,0:T(8,128)(2,1)S(1)} async-done(((bf16[4,4,2,128,2,128]{5,3,4,2,1,0:T(8,128)(2,1)}), bf16[4,4,2,128,2,128]{5,3,4,2,1,0:T(8,128)(2,1)S(1)}, u32[]{:S(2)}, u32[]{:S(2)}) %all-to-all-start.3) | async-done | bytes 2097184 | tf_op jit(solution)/shard_map/all_to_all | solution.py:85
  117.2 1.7 %gather_fusion.1 = bf16[8,2,128,2,128]{4,2,3,1,0:T(8,128)(2,1)} fusion(bf16[16,2,128,2,128]{4,2,3,1,0:T(8,128)(2,1)S(1)} %bitcast.111, s32[1024]{0:T(1024)S(1)} %pad_clamp_fusion.1), kind=kCustom, calls=%fused_computation.1 | custom fusion | bytes 2097184 | tf_op jit(solution)/shard_map/jit(_take)/gather | solution.py:86
  118.9 1.4 copy_select_fusion.1
  120.3 0.5 fusion.41
  120.8 0.3 convolution_bitcast_fusion
  121.1 0.2 fusion.16
  121.5 0.2 fusion.13
  121.8 0.1 multiply_reduce_fusion.1
  121.9 0.6 gather_fusion.2
  122.6 5.7 %psum.14 = f32[8]{0:T(128)S(1)} all-reduce(f32[8]{0:T(128)S(1)} %multiply_reduce_fusion.1), channel_id=1, replica_groups=mesh['parts'=2,'dp'=4,'tensor'=4] {'tensor'}, use_global_device_ids=true, to_apply=%region_12.13 | all-reduce | flops 8 | bytes 64 | tf_op jit(solution)/shard_map/psum | solution.py:149
  128.2 0.6 fusion.34
  128.8 16.2 %pmax.7 = f32[]{:T(128)} all-reduce(f32[]{:T(128)} %get-tuple-element.16), channel_id=1, replica_groups=mesh['parts'=2,'dp'=4,'tensor'=4] {'dp'}, use_global_device_ids=true, to_apply=%region_14.15 | all-reduce | flops 1 | bytes 8 | tf_op jit(solution)/shard_map/pmax | solution.py:151
  145.0 1.3 exponential_reduce_fusion
  146.3 9.1 %psum.15 = f32[]{:T(128)} all-reduce(f32[]{:T(128)} %exponential_reduce_fusion), channel_id=1, replica_groups=mesh['parts'=2,'dp'=4,'tensor'=4] {'dp'}, use_global_device_ids=true, to_apply=%region_16.17 | all-reduce | flops 1 | bytes 8 | tf_op jit(solution)/shard_map/psum | solution.py:152
  156.8 0.5 broadcast_subtract_fusion
  (48 shorter events, 1.0 us)
Async XLA Ops:
  0.6 60.8 %copy-start = (bf16[8,2,128,2,128]{4,3,2,1,0:T(2,128)(2,1)S(1)}, bf16[8,2,128,2,128]{4,3,2,1,0:T(2,128)(2,1)}, u32[]{:S(2)}) copy-start(bf16[8,2,128,2,128]{4,3,2,1,0:T(2,128)(2,1)} %param.8) | copy-start | bytes 3145732
  2.4 32.9 %all-to-all-start.2 = ((s32[4,1,4]{2,1,0:T(1,128)}), s32[4,1,4]{2,1,0:T(1,128)S(1)}, u32[]{:S(2)}, u32[]{:S(2)}) async-start(s32[4,1,4]{2,1,0:T(1,128)} %bitcast.10), calls=%async_computation.2 | async-start | bytes 4096 | tf_op jit(solution)/shard_map/all_to_all | solution.py:77
  35.3 11.3 %all-to-all-start.1 = ((f32[4,1,256]{2,1,0:T(1,128)}), f32[4,1,256]{2,1,0:T(1,128)S(1)}, u32[]{:S(2)}, u32[]{:S(2)}) async-start(f32[4,1,256]{2,1,0:T(1,128)} %reshape.241), calls=%async_computation.1 | async-start | bytes 8192 | tf_op jit(solution)/shard_map/all_to_all | solution.py:122
  44.6 30.9 %copy-start.3 = (bf16[2,2,8,2,128]{4,3,2,1,0:T(2,128)(2,1)S(1)}, bf16[2,2,8,2,128]{4,3,2,1,0:T(2,128)(2,1)}, u32[]{:S(2)}) copy-start(bf16[2,2,8,2,128]{4,3,2,1,0:T(2,128)(2,1)} %param.10) | copy-start | bytes 49156
  44.6 30.9 %copy-start.2 = (bf16[2,8,16,128]{3,2,1,0:T(8,128)(2,1)S(1)}, bf16[2,8,16,128]{3,2,1,0:T(8,128)(2,1)}, u32[]{:S(2)}) copy-start(bf16[2,8,16,128]{3,2,1,0:T(8,128)(2,1)} %param.9) | copy-start | bytes 196612
  45.7 30.5 %copy-start.7 = (u32[32]{0:T(128)S(1)}, u32[32]{0:T(128)}, u32[]{:S(2)}) copy-start(u32[32]{0:T(128)} %constant.108) | copy-start | bytes 388
  45.7 31.8 %copy-start.6 = (f32[8]{0:T(128)S(1)}, f32[8]{0:T(128)}, u32[]{:S(2)}) copy-start(f32[8]{0:T(128)} %param.12) | copy-start | bytes 100
  46.6 10.7 %all-to-all-start.4 = ((f32[4,1,256]{2,1,0:T(1,128)}), f32[4,1,256]{2,1,0:T(1,128)S(1)}, u32[]{:S(2)}, u32[]{:S(2)}) async-start(f32[4,1,256]{2,1,0:T(1,128)} %reshape.243), calls=%async_computation.4 | async-start | bytes 8192 | tf_op jit(solution)/shard_map/all_to_all | solution.py:129
  57.3 14.6 %all-to-all-start = ((f32[2,4,8,16,128]{4,3,2,0,1:T(8,128)}), f32[2,4,8,16,128]{4,3,2,0,1:T(8,128)}, u32[]{:S(2)}, u32[]{:S(2)}) async-start(f32[2,4,8,16,128]{4,3,2,0,1:T(8,128)} %copy.104), calls=%async_computation | async-start | bytes 1048576 | tf_op jit(solution)/shard_map/all_to_all | solution.py:136
  68.2 53.6 %copy-start.4 = (f32[16,128]{1,0:T(8,128)S(1)}, f32[16,128]{1,0:T(8,128)}, u32[]{:S(2)}) copy-start(f32[16,128]{1,0:T(8,128)} %param.13) | copy-start | bytes 24580
  68.2 60.0 %copy-start.5 = (s32[8]{0:T(128)S(1)}, s32[8]{0:T(128)}, u32[]{:S(2)}) copy-start(s32[8]{0:T(128)} %param.11) | copy-start | bytes 100
  71.9 45.4 %all-to-all-start.3 = ((bf16[4,4,2,128,2,128]{5,3,4,2,1,0:T(8,128)(2,1)}), bf16[4,4,2,128,2,128]{5,3,4,2,1,0:T(8,128)(2,1)S(1)}, u32[]{:S(2)}, u32[]{:S(2)}) async-start(bf16[4,4,2,128,2,128]{5,3,4,2,1,0:T(8,128)(2,1)} %copy_select_fusion), calls=%async_computation.3 | async-start | bytes 4194304 | tf_op jit(solution)/shard_map/all_to_all | solution.py:85
  121.8 35.5 %copy-start.1 = (bf16[2,8,16,128]{3,2,1,0:T(8,128)(2,1)}, bf16[2,8,16,128]{3,2,1,0:T(8,128)(2,1)S(1)}, u32[]{:S(2)}) copy-start(bf16[2,8,16,128]{3,2,1,0:T(8,128)(2,1)S(1)} %fusion.13) | copy-start | bytes 196612
where the time goes:
time: 158 us; the launch traced here: 157 us
  blocking collectives  76.7 us (49%)
  starting transfers between devices  24 us (15%)
  local copies, waits for them, and re-layouts  15.5 us (10%)
  other arithmetic  14.3 us (9%)
  waiting for transfers between devices  13.8 us (9%)
  matrix products  9.94 us (6%)
  between operations  2.94 us (2%)
    unnamed x1, blocking collectives  31.2 us
    pmax x1, blocking collectives, per_device(): largest_weight = lax.pmax(jnp.max(raw_weight), 'dp')  16.2 us
    all_gather x1, blocking collectives, per_device(): everyone = lax.all_gather(queries, 'dp', axis=1, tiled=True)  14.6 us
    psum x1, blocking collectives, per_device(): weight_mass = lax.psum(jnp.sum(jnp.exp(raw_weight - largest_weight)), 'dp')  9.05 us
    all_to_all x1, starting transfers between devices, per_device(): lax.all_to_all(wanted.reshape(devices, capacity), 'dp', split_axis=0, con...  6.35 us
    psum x1, blocking collectives, per_device(): twist_value = lax.psum(local_twist, 'tensor')  5.66 us
    all_to_all x1, waiting for transfers between devices, per_device(): lax.all_to_all(totals.reshape(step_count, devices, local_count, head_coun...  5.47 us
    all_to_all x1, starting transfers between devices, per_device(): lax.all_to_all(totals.reshape(step_count, devices, local_count, head_coun...  5.09 us
  transfers between devices with their start and end apart: 5, of which 3 were waited for; matrix products, arithmetic and copies ran while one was open for 19% of the time, Pallas kernels for 0%

commit v1 on v0

--- a/solution.py
+++ b/solution.py
@@ -111,7 +111,16 @@
         totals.reshape(step_count, local_count, head_count),
         weighted.reshape(step_count, local_count, head_count, head_size),
     )
-    everyone = lax.all_gather(queries, "dp", axis=1, tiled=True)
+    ways = lax.axis_size("dp")
+    up = [(d, (d + 1) % ways) for d in range(ways)]
+    down = [(d, (d - 1) % ways) for d in range(ways)]
+    earlier_2, later = ([queries], [queries])
+    for _ in range(ways // 2):
+        earlier_2.append(lax.ppermute(earlier_2[-1], "dp", up))
+    for _ in range((ways - 1) // 2):
+        later.append(lax.ppermute(later[-1], "dp", down))
+    line = jnp.concatenate([*earlier_2[::-1], *later[1:]], axis=1)
+    everyone = jnp.roll(line, (lax.axis_index("dp") - ways // 2) * queries.shape[1], axis=1)
     largest, totals, weighted = prompt_states(
         everyone.reshape(step_count * devices * local_count, head_count, head_size),
         prompt_kv,

time: 158 us -> 151 us (0.956)
  blocking collectives: 76.7 us -> 65.9 us
  local copies, waits for them, and re-layouts: 15.5 us -> 20.1 us
  other arithmetic: 14.3 us -> 11.2 us
  starting transfers between devices: 24 us -> 27.1 us
  matrix products: 9.94 us -> 6.93 us
  waiting for transfers between devices: 13.8 us -> 15.6 us
    all_gather x1 -> x0, blocking collectives: 14.6 us -> none  [per_device(): everyone = lax.all_gather(queries, 'dp', axis=1, tiled=True)]
    ppermute x0 -> x3, starting transfers between devices: none -> 7.16 us  [the longest x1 5.13 us: per_device(): later.append(lax.ppermute(later[-1], 'dp', down))]
    unnamed x23 -> x32, local copies, waits for them, and re-layouts: 2.39 us -> 7.14 us
    unnamed x1, blocking collectives: 31.2 us -> 35 us
    reduce_sum x3, other arithmetic: 4.73 us -> 1.64 us  [block_state(): return (largest, jnp.sum(exponent, axis=-1), weighted)]
    dot_general x1, matrix products: 4.1 us -> 1.2 us  [attend_block(): jnp.einsum('pcgd,kcd->pcgk', query_block, key_rows, preferred_element_typ...]
    all_to_all x1, starting transfers between devices: 5.09 us -> 3.25 us  [per_device(): lax.all_to_all(totals.reshape(step_count, devices, local_count, head_coun...]
    ppermute x0 -> x3, waiting for transfers between devices: none -> 1.7 us  [the longest x2 1.7 us: per_device(): earlier_2.append(lax.ppermute(earlier_2[-1], 'dp', up))]
  transfers between devices with their start and end apart: 5 -> 8, of which waited for: 3 -> 5; matrix products, arithmetic and copies ran while one was open for 19% -> 18% of each run, Pallas kernels for 0% -> 0%
where the time goes in v1:
time: 151 us; the launch traced here: 150 us
  blocking collectives  65.9 us (44%)
  starting transfers between devices  27.1 us (18%)
  local copies, waits for them, and re-layouts  20.1 us (13%)
  waiting for transfers between devices  15.6 us (10%)
  other arithmetic  11.2 us (7%)
  matrix products  6.93 us (5%)
  between operations  3.03 us (2%)
    unnamed x1, blocking collectives  35 us
    pmax x1, blocking collectives, per_device(): largest_weight = lax.pmax(jnp.max(raw_weight), 'dp')  16 us
    psum x1, blocking collectives, per_device(): weight_mass = lax.psum(jnp.sum(jnp.exp(raw_weight - largest_weight)), 'dp')  9.05 us
    unnamed x32, local copies, waits for them, and re-layouts  7.14 us
    psum x1, blocking collectives, per_device(): twist_value = lax.psum(local_twist, 'tensor')  5.82 us
    ppermute x1, starting transfers between devices, per_device(): later.append(lax.ppermute(later[-1], 'dp', down))  5.13 us
    all_to_all x1, starting transfers between devices, per_device(): lax.all_to_all(wanted.reshape(devices, capacity), 'dp', split_axis=0, con...  5.09 us
    gather x1, local copies, waits for them, and re-layouts, per_device(): jnp.take(gen_kv, picked, axis=0)  5.09 us
  transfers between devices with their start and end apart: 8, of which 5 were waited for; matrix products, arithmetic and copies ran while one was open for 18% of the time, Pallas kernels for 0%

profile of v1, /device:TPU:0, one launch (start us, length us, event | category | flops | bytes accessed | tf_op | source)
XLA Modules:
  0.0 149.9 jit_solution(12539336047507572728)
XLA Ops:
  0.6 5.1 %collective-permute-start.2 = (bf16[2,8,16,128]{3,2,1,0:T(8,128)(2,1)}, bf16[2,8,16,128]{3,2,1,0:T(8,128)(2,1)S(1)}, u32[]{:S(2)}, u32[]{:S(2)}) collective-permute-start(bf16[2,8,16,128]{3,2,1,0:T(8,128)(2,1)} %param.9), channel_id=1, source_target_pairs={{0,12},{4,0},{8,4},{12,8},{1,13},{5,1},{9,5},{13,9},{2,14},{6,2},{... | collective-permute-start | bytes 196616 | tf_op jit(solution)/shard_map/ppermute | solution.py:121
  5.8 0.7 compare_select_fusion.3
  6.7 0.7 sub.115
  7.4 5.1 %all-to-all-start.2 = ((s32[4,1,4]{2,1,0:T(1,128)}), s32[4,1,4]{2,1,0:T(1,128)S(1)}, u32[]{:S(2)}, u32[]{:S(2)}) async-start(s32[4,1,4]{2,1,0:T(1,128)} %bitcast.10), calls=%async_computation.2 | async-start | bytes 4096 | tf_op jit(solution)/shard_map/all_to_all | solution.py:77
  12.5 2.0 %collective-permute-start.1 = (bf16[2,8,16,128]{3,2,1,0:T(8,128)(2,1)S(1)}, bf16[2,8,16,128]{3,2,1,0:T(8,128)(2,1)S(1)}, u32[]{:S(2)}, u32[]{:S(2)}) collective-permute-start(bf16[2,8,16,128]{3,2,1,0:T(8,128)(2,1)S(1)} %collective-permute-done), channel_id=1, source_target_pairs={{0,4},{4,8},{8,12},{12,0},{1,5},{5,9},{9,13},{13,1},{2,6},{6,10},{... | collective-permute-start | bytes 196616 | tf_op jit(solution)/shard_map/ppermute | solution.py:119
  14.5 2.5 %fusion.42 = (bf16[1,1792,2,128]{3,2,1,0:T(2,128)(2,1)S(1)}, bf16[1,1792,2,128]{3,2,1,0:T(2,128)(2,1)S(1)}) fusion(bf16[2,1792,2,128]{3,2,1,0:T(2,128)(2,1)} %param.7), kind=kLoop, calls=%fused_computation.99 | loop fusion | bytes 3670016 | tf_op jit(solution)/shard_map/slice | solution.py:44
  17.0 1.7 %collective-permute-done.1 = bf16[2,8,16,128]{3,2,1,0:T(8,128)(2,1)S(1)} collective-permute-done((bf16[2,8,16,128]{3,2,1,0:T(8,128)(2,1)S(1)}, bf16[2,8,16,128]{3,2,1,0:T(8,128)(2,1)S(1)}, u32[]{:S(2)}, u32[]{:S(2)}) %collective-permute-start.1) | collective-permute-done | bytes 65568 | tf_op jit(solution)/shard_map/ppermute | solution.py:119
  18.7 0.9 constant_dynamic-update-slice_fusion.5
  19.6 0.9 constant_dynamic-update-slice_fusion.1
  20.6 1.2 bitcast_reduce_fusion
  21.8 3.0 %copy-done.1 = f32[2,64,8,1792]{3,2,1,0:T(8,128)} copy-done((f32[2,64,8,1792]{3,2,1,0:T(8,128)}, f32[2,64,8,1792]{3,2,1,0:T(8,128)S(1)}, u32[]{:S(2)}) %copy-start.1) | copy-done | bytes 7340056
  24.7 1.3 fusion.1
  26.3 0.7 reshape.243
  27.0 3.2 %all-to-all-start.4 = ((f32[4,1,256]{2,1,0:T(1,128)}), f32[4,1,256]{2,1,0:T(1,128)S(1)}, u32[]{:S(2)}, u32[]{:S(2)}) async-start(f32[4,1,256]{2,1,0:T(1,128)} %reshape.243), calls=%async_computation.4 | async-start | bytes 8192 | tf_op jit(solution)/shard_map/all_to_all | solution.py:138
  30.6 0.7 reshape.241
  31.3 4.3 %all-to-all-done.4 = f32[4,1,256]{2,1,0:T(1,128)S(1)} async-done(((f32[4,1,256]{2,1,0:T(1,128)}), f32[4,1,256]{2,1,0:T(1,128)S(1)}, u32[]{:S(2)}, u32[]{:S(2)}) %all-to-all-start.4) | async-done | bytes 4128 | tf_op jit(solution)/shard_map/all_to_all | solution.py:138
  35.7 3.2 %all-to-all-start.1 = ((f32[4,1,256]{2,1,0:T(1,128)}), f32[4,1,256]{2,1,0:T(1,128)S(1)}, u32[]{:S(2)}, u32[]{:S(2)}) async-start(f32[4,1,256]{2,1,0:T(1,128)} %reshape.241), calls=%async_computation.1 | async-start | bytes 8192 | tf_op jit(solution)/shard_map/all_to_all | solution.py:131
  38.9 4.3 %fusion.7 = f32[64,2,8,128]{3,2,0,1:T(8,128)S(1)} fusion(f32[2,64,8,1792]{3,2,1,0:T(8,128)} %copy-done.1, f32[64,2,8]{2,0,1:T(8,128)S(1)} %get-tuple-element.47, bf16[1,1792,2,128]{3,2,1,0:T(2,128)(2,1)S(1)} %get-tuple-element.34), kind=kOutput, calls=%fused_computation.12 | convolution fusion | flops 475267072 | bytes 8785920 | tf_op jit(solution)/shard_map/while/body/eval_jaxpr/pcgk,kcd->pcgd/dot_general | solution.py:32
  43.3 0.8 copy.104
  44.2 0.3 all-to-all-done.1
  44.5 4.8 %all-to-all-start = ((f32[2,4,8,16,128]{4,3,2,0,1:T(8,128)}), f32[2,4,8,16,128]{4,3,2,0,1:T(8,128)}, u32[]{:S(2)}, u32[]{:S(2)}) async-start(f32[2,4,8,16,128]{4,3,2,0,1:T(8,128)} %copy.104), calls=%async_computation | async-start | bytes 1048576 | tf_op jit(solution)/shard_map/all_to_all | solution.py:145
  49.3 5.1 %gather_fusion = bf16[16,2,128,2,128]{4,3,2,1,0:T(2,128)(2,1)S(1)} fusion(bf16[8,2,128,2,128]{4,3,2,1,0:T(2,128)(2,1)S(1)} %copy-done, s32[1024]{0:T(1024)S(1)} %pad_clamp_fusion.2), kind=kCustom, calls=%fused_computation | custom fusion | bytes 4194368 | tf_op jit(solution)/shard_map/jit(_take)/gather | solution.py:84
  54.4 1.7 %copy_select_fusion = bf16[4,4,2,128,2,128]{5,3,4,2,1,0:T(8,128)(2,1)} fusion(bf16[4,4,2,128,2,128]{5,4,3,2,1,0:T(2,128)(2,1)S(1)} %bitcast.111, pred[4,4]{1,0:T(4,128)(4,1)S(1)} %compare_and_fusion), kind=kLoop, calls=%fused_computation.11 | loop fusion | flops 1048576 | bytes 4194320 | tf_op jit(solution)/shard_map/jit(_take)/select_n | solution.py:84
  56.0 4.5 %all-to-all-done = f32[2,4,8,16,128]{4,3,2,0,1:T(8,128)} async-done(((f32[2,4,8,16,128]{4,3,2,0,1:T(8,128)}), f32[2,4,8,16,128]{4,3,2,0,1:T(8,128)}, u32[]{:S(2)}, u32[]{:S(2)}) %all-to-all-start) | async-done | bytes 524320 | tf_op jit(solution)/shard_map/all_to_all | solution.py:145
  60.6 3.6 %all-to-all-start.3 = ((bf16[4,4,2,128,2,128]{5,3,4,2,1,0:T(8,128)(2,1)}), bf16[4,4,2,128,2,128]{5,3,4,2,1,0:T(8,128)(2,1)S(1)}, u32[]{:S(2)}, u32[]{:S(2)}) async-start(bf16[4,4,2,128,2,128]{5,3,4,2,1,0:T(8,128)(2,1)} %copy_select_fusion), calls=%async_computation.3 | async-start | bytes 4194304 | tf_op jit(solution)/shard_map/all_to_all | solution.py:85
  64.3 0.4 fusion.44
  64.9 0.6 dynamic-slice
  66.2 0.2 dynamic-update-slice
  66.4 35.0 %all-reduce = f32[32]{0:T(128)S(1)} all-reduce(f32[32]{0:T(128)S(1)} %dynamic-update-slice), channel_id=1, replica_groups=mesh['parts'=2,'dp'=4,'tensor'=4] {'dp'}, use_global_device_ids=true, to_apply=%add | all-reduce | flops 32 | bytes 256
  101.5 0.2 convolution_bitcast_fusion.1
  101.7 0.5 broadcast.207
  102.3 0.7 reduce.5
  103.0 0.7 reduce.4
  103.8 1.3 multiply_reduce_fusion
  105.1 4.8 %all-to-all-done.3 = bf16[4,4,2,128,2,128]{5,3,4,2,1,0:T(8,128)(2,1)S(1)} async-done(((bf16[4,4,2,128,2,128]{5,3,4,2,1,0:T(8,128)(2,1)}), bf16[4,4,2,128,2,128]{5,3,4,2,1,0:T(8,128)(2,1)S(1)}, u32[]{:S(2)}, u32[]{:S(2)}) %all-to-all-start.3) | async-done | bytes 2097184 | tf_op jit(solution)/shard_map/all_to_all | solution.py:85
  109.8 1.7 %gather_fusion.1 = bf16[8,2,128,2,128]{4,2,3,1,0:T(8,128)(2,1)} fusion(bf16[16,2,128,2,128]{4,2,3,1,0:T(8,128)(2,1)S(1)} %bitcast.112, s32[1024]{0:T(1024)S(1)} %pad_clamp_fusion.1), kind=kCustom, calls=%fused_computation.1 | custom fusion | bytes 2097184 | tf_op jit(solution)/shard_map/jit(_take)/gather | solution.py:86
  111.5 1.4 copy_select_fusion.1
  112.9 0.5 fusion.45
  113.4 0.3 convolution_bitcast_fusion
  113.7 0.2 fusion.20
  114.1 0.2 fusion.17
  114.5 0.6 gather_fusion.2
  115.2 5.8 %psum.14 = f32[8]{0:T(128)S(1)} all-reduce(f32[8]{0:T(128)S(1)} %multiply_reduce_fusion.1), channel_id=1, replica_groups=mesh['parts'=2,'dp'=4,'tensor'=4] {'tensor'}, use_global_device_ids=true, to_apply=%region_12.13 | all-reduce | flops 8 | bytes 64 | tf_op jit(solution)/shard_map/psum | solution.py:158
  121.0 0.6 fusion.38
  121.6 16.0 %pmax.7 = f32[]{:T(128)} all-reduce(f32[]{:T(128)} %get-tuple-element.16), channel_id=1, replica_groups=mesh['parts'=2,'dp'=4,'tensor'=4] {'dp'}, use_global_device_ids=true, to_apply=%region_14.15 | all-reduce | flops 1 | bytes 8 | tf_op jit(solution)/shard_map/pmax | solution.py:160
  137.6 1.3 exponential_reduce_fusion
  138.9 9.1 %psum.15 = f32[]{:T(128)} all-reduce(f32[]{:T(128)} %exponential_reduce_fusion), channel_id=1, replica_groups=mesh['parts'=2,'dp'=4,'tensor'=4] {'dp'}, use_global_device_ids=true, to_apply=%region_16.17 | all-reduce | flops 1 | bytes 8 | tf_op jit(solution)/shard_map/psum | solution.py:161
  149.3 0.5 broadcast_subtract_fusion
  (66 shorter events, 2.0 us)
Async XLA Ops:
  0.6 48.6 %copy-start = (bf16[8,2,128,2,128]{4,3,2,1,0:T(2,128)(2,1)S(1)}, bf16[8,2,128,2,128]{4,3,2,1,0:T(2,128)(2,1)}, u32[]{:S(2)}) copy-start(bf16[8,2,128,2,128]{4,3,2,1,0:T(2,128)(2,1)} %param.8) | copy-start | bytes 3145732
  0.6 18.9 %collective-permute-start.2 = (bf16[2,8,16,128]{3,2,1,0:T(8,128)(2,1)}, bf16[2,8,16,128]{3,2,1,0:T(8,128)(2,1)S(1)}, u32[]{:S(2)}, u32[]{:S(2)}) collective-permute-start(bf16[2,8,16,128]{3,2,1,0:T(8,128)(2,1)} %param.9), channel_id=1, source_target_pairs={{0,12},{4,0},{8,4},{12,8},{1,13},{5,1},{9,5},{13,9},{2,14},{6,2},{... | collective-permute-start | bytes 196616 | tf_op jit(solution)/shard_map/ppermute | solution.py:121
  5.8 6.7 %collective-permute-start = (bf16[2,8,16,128]{3,2,1,0:T(8,128)(2,1)}, bf16[2,8,16,128]{3,2,1,0:T(8,128)(2,1)S(1)}, u32[]{:S(2)}, u32[]{:S(2)}) collective-permute-start(bf16[2,8,16,128]{3,2,1,0:T(8,128)(2,1)} %param.9), channel_id=1, source_target_pairs={{0,4},{4,8},{8,12},{12,0},{1,5},{5,9},{9,13},{13,1},{2,6},{6,10},{... | collective-permute-start | bytes 196616 | tf_op jit(solution)/shard_map/ppermute | solution.py:119
  7.4 19.6 %all-to-all-start.2 = ((s32[4,1,4]{2,1,0:T(1,128)}), s32[4,1,4]{2,1,0:T(1,128)S(1)}, u32[]{:S(2)}, u32[]{:S(2)}) async-start(s32[4,1,4]{2,1,0:T(1,128)} %bitcast.10), calls=%async_computation.2 | async-start | bytes 4096 | tf_op jit(solution)/shard_map/all_to_all | solution.py:77
  12.5 6.2 %collective-permute-start.1 = (bf16[2,8,16,128]{3,2,1,0:T(8,128)(2,1)S(1)}, bf16[2,8,16,128]{3,2,1,0:T(8,128)(2,1)S(1)}, u32[]{:S(2)}, u32[]{:S(2)}) collective-permute-start(bf16[2,8,16,128]{3,2,1,0:T(8,128)(2,1)S(1)} %collective-permute-done), channel_id=1, source_target_pairs={{0,4},{4,8},{8,12},{12,0},{1,5},{5,9},{9,13},{13,1},{2,6},{6,10},{... | collective-permute-start | bytes 196616 | tf_op jit(solution)/shard_map/ppermute | solution.py:119
  21.8 3.0 %copy-start.1 = (f32[2,64,8,1792]{3,2,1,0:T(8,128)}, f32[2,64,8,1792]{3,2,1,0:T(8,128)S(1)}, u32[]{:S(2)}) copy-start(f32[2,64,8,1792]{3,2,1,0:T(8,128)S(1)} %get-tuple-element.48) | copy-start | bytes 22020100
  27.0 8.6 %all-to-all-start.4 = ((f32[4,1,256]{2,1,0:T(1,128)}), f32[4,1,256]{2,1,0:T(1,128)S(1)}, u32[]{:S(2)}, u32[]{:S(2)}) async-start(f32[4,1,256]{2,1,0:T(1,128)} %reshape.243), calls=%async_computation.4 | async-start | bytes 8192 | tf_op jit(solution)/shard_map/all_to_all | solution.py:138
  35.7 8.8 %all-to-all-start.1 = ((f32[4,1,256]{2,1,0:T(1,128)}), f32[4,1,256]{2,1,0:T(1,128)S(1)}, u32[]{:S(2)}, u32[]{:S(2)}) async-start(f32[4,1,256]{2,1,0:T(1,128)} %reshape.241), calls=%async_computation.1 | async-start | bytes 8192 | tf_op jit(solution)/shard_map/all_to_all | solution.py:131
  43.3 20.9 %copy-start.4 = (bf16[2,2,8,2,128]{4,3,2,1,0:T(2,128)(2,1)S(1)}, bf16[2,2,8,2,128]{4,3,2,1,0:T(2,128)(2,1)}, u32[]{:S(2)}) copy-start(bf16[2,2,8,2,128]{4,3,2,1,0:T(2,128)(2,1)} %param.10) | copy-start | bytes 49156
  43.3 20.9 %copy-start.2 = (bf16[2,8,16,128]{3,2,1,0:T(8,128)(2,1)S(1)}, bf16[2,8,16,128]{3,2,1,0:T(8,128)(2,1)}, u32[]{:S(2)}) copy-start(bf16[2,8,16,128]{3,2,1,0:T(8,128)(2,1)} %param.9) | copy-start | bytes 196612
  43.3 21.6 %copy-start.8 = (u32[32]{0:T(128)S(1)}, u32[32]{0:T(128)}, u32[]{:S(2)}) copy-start(u32[32]{0:T(128)} %constant.135) | copy-start | bytes 388
  43.3 22.9 %copy-start.7 = (f32[8]{0:T(128)S(1)}, f32[8]{0:T(128)}, u32[]{:S(2)}) copy-start(f32[8]{0:T(128)} %param.12) | copy-start | bytes 100
  44.5 16.1 %all-to-all-start = ((f32[2,4,8,16,128]{4,3,2,0,1:T(8,128)}), f32[2,4,8,16,128]{4,3,2,0,1:T(8,128)}, u32[]{:S(2)}, u32[]{:S(2)}) async-start(f32[2,4,8,16,128]{4,3,2,0,1:T(8,128)} %copy.104), calls=%async_computation | async-start | bytes 1048576 | tf_op jit(solution)/shard_map/all_to_all | solution.py:145
  56.0 58.4 %copy-start.5 = (f32[16,128]{1,0:T(8,128)S(1)}, f32[16,128]{1,0:T(8,128)}, u32[]{:S(2)}) copy-start(f32[16,128]{1,0:T(8,128)} %param.13) | copy-start | bytes 24580
  56.0 65.0 %copy-start.6 = (s32[8]{0:T(128)S(1)}, s32[8]{0:T(128)}, u32[]{:S(2)}) copy-start(s32[8]{0:T(128)} %param.11) | copy-start | bytes 100
  60.6 49.3 %all-to-all-start.3 = ((bf16[4,4,2,128,2,128]{5,3,4,2,1,0:T(8,128)(2,1)}), bf16[4,4,2,128,2,128]{5,3,4,2,1,0:T(8,128)(2,1)S(1)}, u32[]{:S(2)}, u32[]{:S(2)}) async-start(bf16[4,4,2,128,2,128]{5,3,4,2,1,0:T(8,128)(2,1)} %copy_select_fusion), calls=%async_computation.3 | async-start | bytes 4194304 | tf_op jit(solution)/shard_map/all_to_all | solution.py:85
  114.4 35.5 %copy-start.3 = (bf16[2,8,16,128]{3,2,1,0:T(8,128)(2,1)}, bf16[2,8,16,128]{3,2,1,0:T(8,128)(2,1)S(1)}, u32[]{:S(2)}) copy-start(bf16[2,8,16,128]{3,2,1,0:T(8,128)(2,1)S(1)} %fusion.17) | copy-start | bytes 196612
